TPU v7x, 32 devices: a whole 2x2x4 slice. The times are simulated.
32 devices in a mesh: groups: 2 (over y), space: 4 (over z), clus: 4 (over x, core).
Axes of the slice: x: 2, y: 2, z: 4, core: 2. Of those that a mesh axis runs over, the one named last changes fastest.
Arguments:
- snapshots: bfloat16 [256, 5, 49152], P('groups', None, ('space', 'clus')), parts along dimension 0
- labels: int32 [256], P('groups'), parts along dimension 0, may hold values from 0 to 3, as said below
- start: float32 [256, 16], P('groups'), parts along dimension 0, may hold values from -6 to 6
- successor: int32 [8], P('groups'), parts along dimension 0, may hold values from 0 to 3, as said below
Outputs:
- modes: bfloat16 [8, 16, 5, 49152], P(('groups', 'clus'), None, None, 'space'), parts along dimension 0
- coefficients: float32 [256, 16], P(('groups', 'clus')), parts along dimension 0
- correlations: float32 [8, 16, 16], P(('groups', 'clus')), parts along dimension 0
There are 2 independent parts, one for each index of `groups`. A program takes and returns all parts, laid end to end along the dimension named above; each array names one. Nothing has to cross between parts.
Inputs may be any that keep to these rules, and one draw needn't show every extreme that they name: `labels`: of the 32 snapshots of each aligned block (those of one index of clus), every cluster holds at least 6 and at most 8; in every block some cluster holds exactly 8. Following successor from any cluster visits all 4 clusters once before returning.
All inputs are finite; a program needn't handle non-finite values.
Results may differ from a plain program's by a relative error of at most 0.0045.
Values may be sent and summed in bfloat16 or wider, within the bound.
No kernel may reach another device: no remote copies, remote signals or barrier semaphores. Data moves between devices by JAX's collectives and lax.ppermute only.
A program may use at most 64 MiB of HBM per device.

v0:
```python
import jax
import jax.numpy as jnp
from jax import lax
from jax.sharding import PartitionSpec as P

ITERS = 2


def subspace(gram, member, start):
    basis = member[:, :, None] * start[None, :, :]
    for step in range(ITERS):
        image = (
            member[:, :, None]
            * jnp.einsum("st,ktm->ksm", gram, basis, precision=lax.Precision.HIGHEST)
            + basis
        )
        inner = jnp.einsum("ksm,ksn->kmn", image, image, precision=lax.Precision.HIGHEST)
        lower = jnp.linalg.cholesky(inner)
        basis = lax.linalg.triangular_solve(
            lower, image, left_side=False, lower=True, transpose_a=True
        )
    return basis


def local(snapshots, labels, start, successor):
    count, variables, cells = snapshots.shape
    clusters = lax.axis_size("clus")
    owner = lax.axis_index("clus")
    total_rows = variables * cells * lax.axis_size("space") * clusters
    flat = snapshots.reshape(count, variables * cells)
    partial_value = lax.dot_general(
        flat, flat, (((1,), (1,)), ((), ())), preferred_element_type=jnp.float32
    )
    gram = lax.psum(partial_value, ("space", "clus")) / total_rows
    cluster_ids = jnp.arange(clusters, dtype=jnp.int32)
    member = (labels[None, :] == cluster_ids[:, None]).astype(jnp.float32)
    basis = subspace(gram, member, start)
    picked = jnp.einsum("ks,ksm->sm", member, basis, precision=lax.Precision.HIGHEST)
    snap_dev = count // clusters
    coefficients = lax.dynamic_slice_in_dim(picked, owner * snap_dev, snap_dev, 0)
    rounded = basis.astype(jnp.bfloat16)
    mode_count = rounded.shape[2]
    modes_full = None
    left = jnp.transpose(rounded, (0, 2, 1)).reshape(clusters * mode_count, count)
    modes_full = jnp.dot(left, flat, preferred_element_type=jnp.float32)
    packed = modes_full.astype(jnp.bfloat16).reshape(clusters, mode_count, variables, cells)
    modes_out = lax.all_to_all(packed, "clus", split_axis=0, concat_axis=3, tiled=True)
    select = (successor[:, None] == cluster_ids[None, :]).astype(jnp.float32)
    wide = rounded.astype(jnp.float32)
    partner = jnp.einsum("ab,bsn->asn", select, wide, precision=lax.Precision.HIGHEST)
    image = jnp.einsum("st,atn->asn", gram, partner, precision=lax.Precision.HIGHEST)
    correlations = jnp.einsum("asm,asn->amn", wide, image, precision=lax.Precision.HIGHEST)
    own_correlation = lax.dynamic_slice_in_dim(correlations, owner, 1, 0)
    return (modes_out, coefficients, own_correlation)


def solution(mesh):
    in_specs = (P("groups", None, ("space", "clus")), P("groups"), P("groups", None), P("groups"))
    out_specs = (
        P(("groups", "clus"), None, None, "space"),
        P(("groups", "clus"), None),
        P(("groups", "clus"), None, None),
    )
    return jax.shard_map(local, mesh=mesh, in_specs=in_specs, out_specs=out_specs, check_vma=False)
```

profile of v0, /device:TPU:8, one launch (start us, length us, event | category | flops | bytes accessed | tf_op | source)
XLA Modules:
  0.0 174.2 jit_solution(173776694287602055)
XLA Ops:
  7.2 5.1 %convolution_bitcast_fusion = f32[128,128]{1,0:T(8,128)} fusion(bf16[128,5,3072]{2,0,1:T(8,128)(2,1)} %param.7), kind=kOutput, calls=%fused_computation.1 | convolution fusion | flops 503316480 | bytes 3997696 | tf_op jit(solution)/shard_map/dot_general | solution.py:31
  12.4 6.3 %copy.38 = bf16[128,5,3072]{0,2,1:T(8,128)(2,1)} copy(bf16[128,5,3072]{2,0,1:T(8,128)(2,1)} %param.7) | data formatting | bytes 7864320 | tf_op args[0]
  18.7 82.0 %all-reduce.2.cloned.1.call-done = f32[128,128]{1,0:T(8,128)} async-done(((f32[128,128]{1,0:T(8,128)}), f32[128,128]{1,0:T(8,128)}) %all-reduce.2.cloned.1.call-update) | async-done | bytes 65552 | tf_op jit(solution)/shard_map/psum | solution.py:34
  100.7 1.1 fusion.3
  101.8 0.2 fusion.35
  102.1 5.9 %custom-call.8 = f32[4,16,16]{2,1,0:T(8,128)S(1)} custom-call(f32[4,16,16]{2,1,0:T(8,128)S(1)} %fusion.16), custom_call_target="Cholesky" | custom-call | tf_op jit(solution)/shard_map/jit(cholesky)/cholesky | solution.py:18
  108.2 4.9 %custom-call.9 = f32[4,1,16,16]{2,3,1,0:T(8,128)S(1)} custom-call(f32[4,1,16,16]{3,2,1,0:T(8,128)S(1)} %select_bitcast_fusion.1), custom_call_target="InvertDiagBlocksLowerTriangular" | custom-call | tf_op jit(solution)/shard_map/triangular_solve/custom-call.0 | solution.py:19
  113.1 0.3 convolution_bitcast_fusion.1
  113.4 1.1 fusion.1
  114.5 0.2 fusion.36
  114.7 5.9 %custom-call.10 = f32[4,16,16]{2,1,0:T(8,128)S(1)} custom-call(f32[4,16,16]{2,1,0:T(8,128)S(1)} %fusion.14), custom_call_target="Cholesky" | custom-call | tf_op jit(solution)/shard_map/jit(cholesky)/cholesky | solution.py:18
  120.8 4.9 %custom-call.11 = f32[4,1,16,16]{2,3,1,0:T(8,128)S(1)} custom-call(f32[4,1,16,16]{3,2,1,0:T(8,128)S(1)} %select_bitcast_fusion), custom_call_target="InvertDiagBlocksLowerTriangular" | custom-call | tf_op jit(solution)/shard_map/triangular_solve/custom-call.0 | solution.py:19
  125.7 0.3 bitcast_convert_fusion
  126.0 4.9 %convolution_convert_fusion = bf16[64,15360]{1,0:T(8,128)(2,1)} fusion(bf16[64,128]{1,0:T(8,128)(2,1)S(1)} %bitcast.78, bf16[128,15360]{0,1:T(8,128)(2,1)} %bitcast.75), kind=kOutput, calls=%fused_computation | convolution fusion | flops 252641280 | bytes 5914624 | tf_op jit(solution)/shard_map/dot_general | solution.py:45
  130.9 4.6 %reshape.50 = bf16[4,16,5,3072]{3,2,1,0:T(8,128)(2,1)S(1)} reshape(bf16[64,15360]{1,0:T(8,128)(2,1)} %convolution_convert_fusion) | data formatting | bytes 3932160 | tf_op jit(solution)/shard_map/reshape | solution.py:46
  135.5 2.6 %copy.39 = bf16[4,16,5,3072]{3,1,2,0:T(8,128)(2,1)} copy(bf16[4,16,5,3072]{3,2,1,0:T(8,128)(2,1)S(1)} %reshape.50) | data formatting | bytes 3932160 | tf_op jit(solution)/shard_map/reshape | solution.py:46
  138.1 3.6 %all-to-all-start = ((bf16[4,16,5,3072]{3,1,2,0:T(8,128)(2,1)}), bf16[4,16,5,3072]{3,1,2,0:T(8,128)(2,1)S(1)}, u32[]{:S(2)}, u32[]{:S(2)}) async-start(bf16[4,16,5,3072]{3,1,2,0:T(8,128)(2,1)} %copy.39), calls=%async_computation | async-start | bytes 3932160 | tf_op jit(solution)/shard_map/all_to_all | solution.py:47
  141.7 0.7 constant_dynamic-slice_fusion.1
  142.4 0.2 fusion.22
  142.6 0.2 fusion.4
  142.8 0.1 fusion.37
  143.0 0.6 constant_dynamic-slice_fusion
  143.6 22.4 %all-to-all-done = bf16[4,16,5,3072]{3,1,2,0:T(8,128)(2,1)S(1)} async-done(((bf16[4,16,5,3072]{3,1,2,0:T(8,128)(2,1)}), bf16[4,16,5,3072]{3,1,2,0:T(8,128)(2,1)S(1)}, u32[]{:S(2)}, u32[]{:S(2)}) %all-to-all-start) | async-done | bytes 1966112 | tf_op jit(solution)/shard_map/all_to_all | solution.py:47
  165.9 1.4 copy.52
  (24 shorter events, 0.7 us)
Async XLA Ops:
  7.2 5.2 %copy-start.2 = (s32[128]{0:T(128)S(1)}, s32[128]{0:T(128)}, u32[]{:S(2)}) copy-start(s32[128]{0:T(128)} %param.8) | copy-start | bytes 1540
  7.2 93.5 %all-reduce.2.cloned.1.call-start = ((), (), s32[]{:S(2)}) async-start(), calls=%async_computation.1 | async-start | bytes 131072 | tf_op jit(solution)/shard_map/psum | solution.py:34
  12.4 88.3 %copy-start.1 = (f32[128,16]{0,1:T(8,128)S(1)}, f32[128,16]{0,1:T(8,128)}, u32[]{:S(2)}) copy-start(f32[128,16]{0,1:T(8,128)} %param.9) | copy-start | bytes 24580
  135.5 6.9 %copy-start.3 = (s32[4]{0:T(128)S(1)}, s32[4]{0:T(128)}, u32[]{:S(2)}) copy-start(s32[4]{0:T(128)} %param.10) | copy-start | bytes 52
  135.5 7.1 %copy-start = (f32[128,128]{1,0:T(8,128)S(1)}, f32[128,128]{1,0:T(8,128)}, u32[]{:S(2)}) copy-start(f32[128,128]{1,0:T(8,128)} %all-reduce.2.cloned.1.call-done) | copy-start | bytes 196612
  138.1 27.9 %all-to-all-start = ((bf16[4,16,5,3072]{3,1,2,0:T(8,128)(2,1)}), bf16[4,16,5,3072]{3,1,2,0:T(8,128)(2,1)S(1)}, u32[]{:S(2)}, u32[]{:S(2)}) async-start(bf16[4,16,5,3072]{3,1,2,0:T(8,128)(2,1)} %copy.39), calls=%async_computation | async-start | bytes 3932160 | tf_op jit(solution)/shard_map/all_to_all | solution.py:47
Sparse Core Ops, SparseCore 0:
  12.5 88.1 all-reduce.1
where the time goes:
time: 175 us; the launch traced here: 174 us
  waiting for transfers between devices  104 us (59%)
  other arithmetic  22.1 us (13%)
  local copies, waits for them, and re-layouts  16.3 us (9%)
  between operations  14.2 us (8%)
  matrix products  13.6 us (8%)
  starting transfers between devices  3.64 us (2%)
    psum x1, waiting for transfers between devices, local(): gram = lax.psum(partial_value, ('space', 'clus')) / total_rows  82 us
    all_to_all x1, waiting for transfers between devices, local(): lax.all_to_all(packed, 'clus', split_axis=0, concat_axis=3, tiled=True)  22.4 us
    another operation x7, other arithmetic, subspace(): lower = jnp.linalg.cholesky(inner)  12 us
    another operation x5, other arithmetic, subspace(): lax.linalg.triangular_solve(lower, image, left_side=False, lower=True, tr...  9.99 us
    reshape x2, local copies, waits for them, and re-layouts, local(): modes_full.astype(jnp.bfloat16)  7.12 us
    unnamed x9, local copies, waits for them, and re-layouts  6.29 us
    dot_general x1, matrix products, local(): lax.dot_general(flat, flat, (((1,), (1,)), ((), ())), preferred_element_t...  5.13 us
    dot_general x1, matrix products, local(): modes_full = jnp.dot(left, flat, preferred_element_type=jnp.float32)  4.86 us
  transfers between devices with their start and end apart: 2, of which 2 were waited for; matrix products, arithmetic and copies ran while one was open for 5% of the time, Pallas kernels for 0%

commit v1 on v0

--- a/solution.py
+++ b/solution.py
@@ -31,7 +31,8 @@
     partial_value = lax.dot_general(
         flat, flat, (((1,), (1,)), ((), ())), preferred_element_type=jnp.float32
     )
-    gram = lax.psum(partial_value, ("space", "clus")) / total_rows
+    detail_regions = lambda inner_x: jnp.sum(lax.all_gather(inner_x, ("space", "clus")), 0)
+    gram = detail_regions(partial_value) / total_rows
     cluster_ids = jnp.arange(clusters, dtype=jnp.int32)
     member = (labels[None, :] == cluster_ids[:, None]).astype(jnp.float32)
     basis = subspace(gram, member, start)

time: 175 us -> 127 us (0.73)
  the two profiles are of different devices: /device:TPU:8 before, /device:TPU:0 now
where the time goes in v1:
time: 127 us; the launch traced here: 126 us
  waiting for transfers between devices  56.8 us (45%)
  other arithmetic  23.3 us (18%)
  local copies, waits for them, and re-layouts  16.3 us (13%)
  between operations  14.2 us (11%)
  matrix products  12 us (9%)
  starting transfers between devices  3.64 us (3%)
    all_gather x1, waiting for transfers between devices, local(): lax.all_gather(inner_x, ('space', 'clus'))  34.4 us
    all_to_all x1, waiting for transfers between devices, local(): lax.all_to_all(packed, 'clus', split_axis=0, concat_axis=3, tiled=True)  22.4 us
    another operation x7, other arithmetic, subspace(): lower = jnp.linalg.cholesky(inner)  12 us
    another operation x5, other arithmetic, subspace(): lax.linalg.triangular_solve(lower, image, left_side=False, lower=True, tr...  9.99 us
    reshape x2, local copies, waits for them, and re-layouts, local(): modes_full.astype(jnp.bfloat16)  7.12 us
    unnamed x7, local copies, waits for them, and re-layouts  6.29 us
    dot_general x1, matrix products, local(): lax.dot_general(flat, flat, (((1,), (1,)), ((), ())), preferred_element_t...  5.13 us
    dot_general x1, matrix products, local(): modes_full = jnp.dot(left, flat, preferred_element_type=jnp.float32)  4.86 us
  transfers between devices with their start and end apart: 2, of which 2 were waited for; matrix products, arithmetic and copies ran while one was open for 6% of the time, Pallas kernels for 0%

profile of v1, /device:TPU:0, one launch (start us, length us, event | category | flops | bytes accessed | tf_op | source)
XLA Modules:
  0.0 126.3 jit_solution(17681398155355237147)
XLA Ops:
  7.2 5.1 %convolution_bitcast_fusion = f32[128,128]{1,0:T(8,128)} fusion(bf16[128,5,3072]{2,0,1:T(8,128)(2,1)} %param.7), kind=kOutput, calls=%fused_computation.1 | convolution fusion | flops 503316480 | bytes 3997696 | tf_op jit(solution)/shard_map/dot_general | solution.py:31
  12.4 6.3 %copy.38 = bf16[128,5,3072]{0,2,1:T(8,128)(2,1)} copy(bf16[128,5,3072]{2,0,1:T(8,128)(2,1)} %param.7) | data formatting | bytes 7864320 | tf_op args[0]
  18.7 34.4 %all-gather.3.cloned.1.call-done = f32[2048,128]{1,0:T(8,128)} async-done(((f32[128,128]{1,0:T(8,128)}), f32[2048,128]{1,0:T(8,128)}) %all-gather.3.cloned.1.call-update) | async-done | bytes 1048592 | tf_op jit(solution)/shard_map/all_gather | solution.py:34
  53.1 1.3 %reduce_sum.9 = f32[128,128]{1,0:T(8,128)S(1)} reduce(f32[16,128,128]{2,1,0:T(8,128)} %bitcast.79, f32[]{:T(128)} %constant.40.clone.1), dimensions={0}, to_apply=%region_0.0 | reduce | flops 245760 | bytes 1114116 | tf_op jit(solution)/shard_map/reduce_sum | solution.py:34
  54.4 0.2 fusion.3
  54.7 0.2 fusion.35
  55.0 5.9 %custom-call.8 = f32[4,16,16]{2,1,0:T(8,128)S(1)} custom-call(f32[4,16,16]{2,1,0:T(8,128)S(1)} %fusion.16), custom_call_target="Cholesky" | custom-call | tf_op jit(solution)/shard_map/jit(cholesky)/cholesky | solution.py:18
  61.1 4.9 %custom-call.9 = f32[4,1,16,16]{2,3,1,0:T(8,128)S(1)} custom-call(f32[4,1,16,16]{3,2,1,0:T(8,128)S(1)} %select_bitcast_fusion.1), custom_call_target="InvertDiagBlocksLowerTriangular" | custom-call | tf_op jit(solution)/shard_map/triangular_solve/custom-call.0 | solution.py:19
  66.0 0.3 convolution_bitcast_fusion.1
  66.3 0.2 fusion.1
  66.5 0.2 fusion.36
  66.8 5.9 %custom-call.10 = f32[4,16,16]{2,1,0:T(8,128)S(1)} custom-call(f32[4,16,16]{2,1,0:T(8,128)S(1)} %fusion.14), custom_call_target="Cholesky" | custom-call | tf_op jit(solution)/shard_map/jit(cholesky)/cholesky | solution.py:18
  72.9 4.9 %custom-call.11 = f32[4,1,16,16]{2,3,1,0:T(8,128)S(1)} custom-call(f32[4,1,16,16]{3,2,1,0:T(8,128)S(1)} %select_bitcast_fusion), custom_call_target="InvertDiagBlocksLowerTriangular" | custom-call | tf_op jit(solution)/shard_map/triangular_solve/custom-call.0 | solution.py:19
  77.8 0.3 bitcast_convert_fusion
  78.1 4.9 %convolution_convert_fusion = bf16[64,15360]{1,0:T(8,128)(2,1)} fusion(bf16[64,128]{1,0:T(8,128)(2,1)S(1)} %bitcast.80, bf16[128,15360]{0,1:T(8,128)(2,1)} %bitcast.76), kind=kOutput, calls=%fused_computation | convolution fusion | flops 252641280 | bytes 5914624 | tf_op jit(solution)/shard_map/dot_general | solution.py:46
  83.0 4.6 %reshape.50 = bf16[4,16,5,3072]{3,2,1,0:T(8,128)(2,1)S(1)} reshape(bf16[64,15360]{1,0:T(8,128)(2,1)} %convolution_convert_fusion) | data formatting | bytes 3932160 | tf_op jit(solution)/shard_map/reshape | solution.py:47
  87.5 2.6 %copy.39 = bf16[4,16,5,3072]{3,1,2,0:T(8,128)(2,1)} copy(bf16[4,16,5,3072]{3,2,1,0:T(8,128)(2,1)S(1)} %reshape.50) | data formatting | bytes 3932160 | tf_op jit(solution)/shard_map/reshape | solution.py:47
  90.1 3.6 %all-to-all-start = ((bf16[4,16,5,3072]{3,1,2,0:T(8,128)(2,1)}), bf16[4,16,5,3072]{3,1,2,0:T(8,128)(2,1)S(1)}, u32[]{:S(2)}, u32[]{:S(2)}) async-start(bf16[4,16,5,3072]{3,1,2,0:T(8,128)(2,1)} %copy.39), calls=%async_computation | async-start | bytes 3932160 | tf_op jit(solution)/shard_map/all_to_all | solution.py:48
  93.7 0.7 constant_dynamic-slice_fusion.1
  94.4 0.2 fusion.22
  94.6 0.2 fusion.4
  95.0 0.6 constant_dynamic-slice_fusion
  95.6 22.4 %all-to-all-done = bf16[4,16,5,3072]{3,1,2,0:T(8,128)(2,1)S(1)} async-done(((bf16[4,16,5,3072]{3,1,2,0:T(8,128)(2,1)}), bf16[4,16,5,3072]{3,1,2,0:T(8,128)(2,1)S(1)}, u32[]{:S(2)}, u32[]{:S(2)}) %all-to-all-start) | async-done | bytes 1966112 | tf_op jit(solution)/shard_map/all_to_all | solution.py:48
  118.0 1.4 %copy.52 = bf16[1,4,5,2,8,3072]{5,4,1,3,2,0:T(8,128)(2,1)} copy(bf16[1,4,5,2,8,3072]{5,4,3,2,1,0:T(8,128)(2,1)S(1)} %bitcast.77) | data formatting | bytes 3932160 | tf_op jit(solution)/shard_map/all_to_all | solution.py:48
  (23 shorter events, 0.9 us)
Async XLA Ops:
  7.2 46.0 %all-gather.3.cloned.1.call-start = ((), (), s32[]{:S(2)}) async-start(), calls=%async_computation.1 | async-start | bytes 1114112 | tf_op jit(solution)/shard_map/all_gather | solution.py:34
  12.4 6.3 %copy-start.1 = (s32[128]{0:T(128)S(1)}, s32[128]{0:T(128)}, u32[]{:S(2)}) copy-start(s32[128]{0:T(128)} %param.8) | copy-start | bytes 1540
  12.4 42.1 %copy-start = (f32[128,16]{0,1:T(8,128)S(1)}, f32[128,16]{0,1:T(8,128)}, u32[]{:S(2)}) copy-start(f32[128,16]{0,1:T(8,128)} %param.9) | copy-start | bytes 24580
  87.5 6.9 %copy-start.2 = (s32[4]{0:T(128)S(1)}, s32[4]{0:T(128)}, u32[]{:S(2)}) copy-start(s32[4]{0:T(128)} %param.10) | copy-start | bytes 52
  90.1 27.9 %all-to-all-start = ((bf16[4,16,5,3072]{3,1,2,0:T(8,128)(2,1)}), bf16[4,16,5,3072]{3,1,2,0:T(8,128)(2,1)S(1)}, u32[]{:S(2)}, u32[]{:S(2)}) async-start(bf16[4,16,5,3072]{3,1,2,0:T(8,128)(2,1)} %copy.39), calls=%async_computation | async-start | bytes 3932160 | tf_op jit(solution)/shard_map/all_to_all | solution.py:48
Sparse Core Ops, SparseCore 0:
  12.5 40.6 all-gather.2
